TPU v7x, 128 devices: a whole 4x4x4 slice. The times are simulated.
128 devices in a mesh: ang: 16 (over z_lo, x, core), kslab: 8 (over z_hi, y).
Axes of the slice: x: 4, y: 4, z: 4 (z_hi: 2, z_lo: 2; z = z_hi * 2 + z_lo), core: 2. Of those that a mesh axis runs over, the one named last changes fastest.
Arguments:
- amplitude: bfloat16 [256, 112, 8, 2048], P('ang', None, 'kslab'), may hold values from -6 to 6
- ps_form: bfloat16 [2048, 896], replicated, may hold values from -0.125 to 0.125
- kgrid: float32 [8], replicated, may hold values from 0.1 to 3
- l_atom: int32 [112], replicated, may hold values from 0 to 7
- l_ps: int32 [112], replicated, may hold values from 0 to 7
- sixj: float32 [8, 12, 8, 8], replicated, may hold values from -0.5 to 0.5
Outputs:
- kernel: float32 [112, 8, 8, 896], P('ang', 'kslab')
All inputs are finite; a program needn't handle non-finite values.
Results may differ from a plain program's by a relative error of at most 0.0003.
Values sent between devices are 32-bit elements; how exact they have to be, the bound alone decides.
No kernel may reach another device: no remote copies, remote signals or barrier semaphores. Data moves between devices by JAX's collectives and lax.ppermute only.
A program may use at most 128 MiB of HBM per device.

v0:
```python
import jax
import jax.numpy as jnp
from jax import lax
from jax.sharding import PartitionSpec as P


def legendre_table(first_row, row_count, total_points, degrees):
    positions = (first_row + jnp.arange(row_count)).astype(jnp.float32)
    angles = jnp.pi * (positions + 0.5) / total_points
    grid_nodes = jnp.cos(angles)
    grid_weights = jnp.pi / total_points * jnp.sin(angles)
    series = [jnp.ones_like(grid_nodes), grid_nodes]
    for degree in range(1, degrees - 1):
        series.append(
            ((2 * degree + 1) * grid_nodes * series[-1] - degree * series[-2]) / (degree + 1)
        )
    return (grid_nodes, grid_weights[None, :] * jnp.stack(series[:degrees]))


def recouple(values, channel_first, j_first, j_count, l_atom, l_ps, sixj, kpoints):
    channel_count = values.shape[0]
    levels = jnp.arange(sixj.shape[2], dtype=jnp.int32)
    atom_levels = lax.dynamic_slice_in_dim(l_atom, channel_first, channel_count)
    onehot_atom = (atom_levels[:, None] == levels[None, :]).astype(jnp.float32)
    onehot_ps = (l_ps[:, None] == levels[None, :]).astype(jnp.float32)
    table = lax.dynamic_slice_in_dim(sixj, j_first, j_count, 0)
    coupling = jnp.einsum(
        "jlxy,ax,by->ajlb", table, onehot_atom, onehot_ps, precision=lax.Precision.HIGHEST
    )
    widened = jnp.repeat(coupling, kpoints, axis=3)
    return jnp.einsum("ajlc,alkc->ajkc", widened, values, precision=lax.Precision.HIGHEST)


def local(amplitude, ps_form, kgrid, l_atom, l_ps, sixj):
    grid_count, channels, slab_points, radial = amplitude.shape
    columns = ps_form.shape[1]
    kpoints = kgrid.shape[0]
    ps_channels = columns // kpoints
    degrees = sixj.shape[1]
    total_j = sixj.shape[0]
    ang_size = lax.axis_size("ang")
    slab_size = lax.axis_size("kslab")
    owned = channels // ang_size
    owned_first = lax.axis_index("ang") * owned
    j_local = total_j // slab_size
    j_first = lax.axis_index("kslab") * j_local
    grid_nodes, projector = legendre_table(
        lax.axis_index("ang") * grid_count, grid_count, grid_count * ang_size, degrees
    )
    krow = lax.dynamic_slice_in_dim(kgrid, lax.axis_index("kslab") * slab_points, slab_points)[
        None, :, None
    ]
    kcol = jnp.tile(kgrid, ps_channels)[None, None, :]
    qinverse = 1.0 / (
        1.0 + krow * krow + kcol * kcol - 2.0 * grid_nodes[:, None, None] * krow * kcol
    )
    intersection = jnp.dot(
        amplitude.reshape(-1, radial), ps_form, preferred_element_type=jnp.float32
    )
    intersection = intersection.reshape(
        grid_count, lax.axis_size("ang") * owned, slab_points, columns
    )
    integrand = intersection * qinverse[:, None]
    summed = lax.psum_scatter(
        jnp.einsum("lg,gakc->alkc", projector, integrand, precision=lax.Precision.HIGHEST),
        "ang",
        scatter_dimension=0,
        tiled=True,
    )
    return recouple(
        lax.all_gather(summed, "kslab", axis=2, tiled=True),
        owned_first,
        j_first,
        j_local,
        l_atom,
        l_ps,
        sixj,
        kpoints,
    )


def solution(mesh):
    in_specs = (P("ang", None, "kslab", None), P(), P(), P(), P(), P())
    out_specs = P("ang", "kslab", None, None)
    return jax.shard_map(local, mesh=mesh, in_specs=in_specs, out_specs=out_specs, check_vma=False)
```

profile of v0, /device:TPU:1, one launch (start us, length us, event | category | flops | bytes accessed | tf_op | source)
XLA Modules:
  0.0 186.4 jit_solution(9028260817376288900)
XLA Ops:
  6.5 0.0 copy-start
  6.5 0.0 reduce-scatter.2.cloned.1.call-start
  6.5 0.1 broadcast_multiply_fusion.1
  6.6 0.1 broadcast_multiply_fusion.3
  6.7 0.1 broadcast_multiply_fusion.5
  6.7 0.1 subtract_multiply_fusion
  6.8 0.1 multiply_cosine_fusion
  6.9 0.1 broadcast_multiply_fusion.7
  6.9 1.2 dynamic_slice.9
  10.2 0.7 tile.2
  10.8 0.1 broadcast_in_dim_tile.3
  11.0 0.1 subtract_divide_fusion
  11.0 21.4 %fusion = f32[16,112,896]{2,0,1:T(8,128)} fusion(bf16[16,112,2048]{2,1,0:T(8,128)(2,1)} %bitcast.36, bf16[2048,896]{1,0:T(8,128)(2,1)} %param.7), kind=kOutput, calls=%fused_computation | convolution fusion | flops 6576668672 | bytes 17432576 | tf_op jit(solution)/shard_map/dot_general | solution.py:57
  32.5 0.1 stack.2
  32.5 9.5 %fusion.6 = f32[112,12,1,896]{3,1,0,2:T(8,128)} fusion(f32[16,112,896]{2,0,1:T(8,128)} %fusion, f32[16,896]{1,0:T(8,128)S(1)} %subtract_divide_fusion, f32[12,16]{1,0:T(8,128)S(1)} %stack.2, f32[16]{0:T(128)S(1)} %get-tuple-element.9), kind=kOutput, calls=%fused_computation.7 | convolution fusion | flops 232816832 | bytes 11297600 | tf_op jit(solution)/shard_map/lg,gakc->alkc/dot_general | solution.py:65
  42.0 0.0 copy-start.2
  42.0 0.0 copy-start.1
  42.0 0.0 reduce-scatter.2.cloned.1.call-update
  42.1 0.2 all-gather.2.cloned.1.call-start
  42.3 70.3 %reduce-scatter.2.cloned.1.call-done = f32[7,12,1,896]{3,1,0,2:T(8,128)} async-done(((f32[112,12,1,896]{3,1,0,2:T(8,128)}), f32[7,12,1,896]{3,1,0,2:T(8,128)}) %reduce-scatter.2.cloned.1.call-update) | async-done | bytes 301072 | tf_op jit(solution)/shard_map/reduce_scatter | solution.py:64
  112.6 1.8 copy.9
  114.4 0.0 all-gather.2.cloned.1.call-update
  114.4 0.0 copy-done.2
  114.4 0.1 dynamic_slice.10
  114.5 0.0 copy-done
  114.5 0.2 fusion.9
  114.7 0.1 copy.13
  114.9 0.0 copy-done.1
  114.9 0.2 fusion.18
  115.1 3.3 %broadcast_in_dim.4 = f32[7,12,112,8]{3,2,0,1:T(8,128)} broadcast(f32[7,12,112]{2,0,1:T(8,128)S(1)} %fusion.18), dimensions={0,1,2} | broadcast | bytes 338688 | tf_op jit(solution)/shard_map/broadcast_in_dim | solution.py:30
  118.4 4.1 %broadcast_in_dim.5 = f32[7,12,896]{2,0,1:T(8,128)S(1)} reshape(f32[7,12,112,8]{3,2,0,1:T(8,128)} %broadcast_in_dim.4) | data formatting | bytes 602112 | tf_op jit(solution)/shard_map/broadcast_in_dim | solution.py:30
  122.4 54.3 %all-gather.2.cloned.1.call-done = f32[7,12,8,896]{3,0,1,2:T(8,128)} async-done(((f32[7,12,1,896]{3,0,1,2:T(8,128)}), f32[7,12,8,896]{3,0,1,2:T(8,128)}) %all-gather.2.cloned.1.call-update) | async-done | bytes 2408464 | tf_op jit(solution)/shard_map/all_gather | solution.py:71
  176.7 2.1 %multiply_reduce_fusion = f32[7,896,8]{1,0,2:T(8,128)S(1)} fusion(f32[7,12,8,896]{3,0,1,2:T(8,128)} %all-gather.2.cloned.1.call-done, f32[7,896,12]{1,0,2:T(8,128)S(1)} %bitcast.35), kind=kLoop, calls=%fused_computation.6 | loop fusion | flops 1154048 | bytes 2910208
  178.8 0.7 copy.32
  (4 shorter events, 0.1 us)
Async XLA Ops:
  6.5 108.0 %copy-start = (f32[8,12,8,8]{1,3,2,0:T(8,128)S(1)}, f32[8,12,8,8]{1,3,2,0:T(8,128)}, u32[]{:S(2)}) copy-start(f32[8,12,8,8]{1,3,2,0:T(8,128)} %param.11) | copy-start | bytes 73732
  6.5 106.0 %reduce-scatter.2.cloned.1.call-start = ((), (), s32[]{:S(2)}) async-start(), calls=%async_computation.1 | async-start | bytes 6823936 | tf_op jit(solution)/shard_map/reduce_scatter | solution.py:64
  42.0 72.4 %copy-start.2 = (s32[112]{0:T(128)S(1)}, s32[112]{0:T(128)}, u32[]{:S(2)}) copy-start(s32[112]{0:T(128)} %param.9) | copy-start | bytes 1348
  42.0 72.8 %copy-start.1 = (s32[112]{0:T(128)S(1)}, s32[112]{0:T(128)}, u32[]{:S(2)}) copy-start(s32[112]{0:T(128)} %param.10) | copy-start | bytes 1348
  42.1 134.7 %all-gather.2.cloned.1.call-start = ((), (), s32[]{:S(2)}) async-start(), calls=%async_computation.2 | async-start | bytes 3096576 | tf_op jit(solution)/shard_map/all_gather | solution.py:71
Sparse Core Ops, SparseCore 0:
  42.2 70.3 reduce-scatter.1
  114.9 61.8 all-gather.1
where the time goes:
time: 187 us; the launch traced here: 186 us
  waiting for transfers between devices  125 us (67%)
  matrix products  31.3 us (17%)
  between operations  15.4 us (8%)
  local copies, waits for them, and re-layouts  12.2 us (7%)
  other arithmetic  2.6 us (1%)
    reduce_scatter x1, waiting for transfers between devices, local(): lax.psum_scatter(jnp.einsum('lg,gakc->alkc', projector, integrand, precis...  70.3 us
    all_gather x1, waiting for transfers between devices, local(): lax.all_gather(summed, 'kslab', axis=2, tiled=True)  54.3 us
    dot_general x1, matrix products, local(): jnp.dot(amplitude.reshape(-1, radial), ps_form, preferred_element_type=jn...  21.4 us
    dot_general x1, matrix products, local(): jnp.einsum('lg,gakc->alkc', projector, integrand, precision=lax.Precision...  9.49 us
    broadcast_in_dim x2, local copies, waits for them, and re-layouts, recouple(): widened = jnp.repeat(coupling, kpoints, axis=3)  7.37 us
  transfers between devices with their start and end apart: 2, of which 2 were waited for; matrix products, arithmetic and copies ran while one was open for 4% of the time, Pallas kernels for 0%

commit v1 on v0

--- a/solution.py
+++ b/solution.py
@@ -2,6 +2,16 @@
 import jax.numpy as jnp
 from jax import lax
 from jax.sharding import PartitionSpec as P
+
+finish_columns = lambda a_name, z_in: jnp.concatenate(
+    lax.all_to_all(
+        jnp.stack([z_in for _ in range(lax.axis_size(a_name))]),
+        axis_name=a_name,
+        split_axis=0,
+        concat_axis=0,
+    ),
+    axis=2,
+)
 
 
 def legendre_table(first_row, row_count, total_points, degrees):
@@ -68,14 +78,7 @@
         tiled=True,
     )
     return recouple(
-        lax.all_gather(summed, "kslab", axis=2, tiled=True),
-        owned_first,
-        j_first,
-        j_local,
-        l_atom,
-        l_ps,
-        sixj,
-        kpoints,
+        finish_columns("kslab", summed), owned_first, j_first, j_local, l_atom, l_ps, sixj, kpoints
     )
 
 

time: 187 us -> 166 us (0.89); the launches traced: 186 us -> 162 us
  waiting for transfers between devices: 125 us -> 94.4 us
  starting transfers between devices: 0.22 us -> 6.46 us
    all_gather x1 -> x0, waiting for transfers between devices: 54.3 us -> none  [local(): lax.all_gather(summed, 'kslab', axis=2, tiled=True)]
    all_to_all x0 -> x1, waiting for transfers between devices: none -> 23.8 us  [lax.all_to_all(jnp.stack([z_in for _ in range(lax.axis_size(a_name))]), a...]
    all_to_all x0 -> x1, starting transfers between devices: none -> 6.46 us  [lax.all_to_all(jnp.stack([z_in for _ in range(lax.axis_size(a_name))]), a...]
    another operation x1 -> x2, local copies, waits for them, and re-layouts: 0.01 us -> 3.7 us  [the longest x1 3.7 us: jnp.stack([z_in for _ in range(lax.axis_size(a_name))])]
    unnamed x1 -> x0, other arithmetic: 2.07 us -> none
  transfers between devices with their start and end apart: 2 -> 2, of which waited for: 2 -> 2; matrix products, arithmetic and copies ran while one was open for 4% -> 5% of each run, Pallas kernels for 0% -> 0%
where the time goes in v1:
time: 166 us; the launch traced here: 162 us
  waiting for transfers between devices  94.4 us (57%)
  matrix products  31.3 us (19%)
  between operations  15.4 us (9%)
  local copies, waits for them, and re-layouts  13.4 us (8%)
  starting transfers between devices  6.46 us (4%)
    reduce_scatter x1, waiting for transfers between devices, local(): lax.psum_scatter(jnp.einsum('lg,gakc->alkc', projector, integrand, precis...  70.5 us
    all_to_all x1, waiting for transfers between devices, lax.all_to_all(jnp.stack([z_in for _ in range(lax.axis_size(a_name))]), a...  23.8 us
    dot_general x1, matrix products, local(): jnp.dot(amplitude.reshape(-1, radial), ps_form, preferred_element_type=jn...  21.4 us
    dot_general x1, matrix products, local(): jnp.einsum('lg,gakc->alkc', projector, integrand, precision=lax.Precision...  9.49 us
    broadcast_in_dim x2, local copies, waits for them, and re-layouts, recouple(): widened = jnp.repeat(coupling, kpoints, axis=3)  7.37 us
    all_to_all x1, starting transfers between devices, lax.all_to_all(jnp.stack([z_in for _ in range(lax.axis_size(a_name))]), a...  6.46 us
    another operation x1, local copies, waits for them, and re-layouts, jnp.stack([z_in for _ in range(lax.axis_size(a_name))])  3.7 us
  transfers between devices with their start and end apart: 2, of which 2 were waited for; matrix products, arithmetic and copies ran while one was open for 5% of the time, Pallas kernels for 0%

profile of v1, /device:TPU:1, one launch (start us, length us, event | category | flops | bytes accessed | tf_op | source)
XLA Modules:
  0.0 162.4 jit_solution(9469897989775629981)
XLA Ops:
  6.5 0.0 copy-start
  6.5 0.0 reduce-scatter.2.cloned.1.call-start
  6.5 0.1 broadcast_multiply_fusion.1
  6.6 0.1 broadcast_multiply_fusion.3
  6.7 0.1 broadcast_multiply_fusion.5
  6.7 0.1 subtract_multiply_fusion
  6.8 0.1 multiply_cosine_fusion
  6.9 0.1 broadcast_multiply_fusion.7
  6.9 1.2 dynamic_slice.9
  10.2 0.7 tile.2
  10.8 0.1 broadcast_in_dim_tile.3
  11.0 0.1 subtract_divide_fusion
  11.0 21.4 %fusion = f32[16,112,896]{2,0,1:T(8,128)} fusion(bf16[16,112,2048]{2,1,0:T(8,128)(2,1)} %bitcast.43, bf16[2048,896]{1,0:T(8,128)(2,1)} %param.7), kind=kOutput, calls=%fused_computation | convolution fusion | flops 6576668672 | bytes 17432576 | tf_op jit(solution)/shard_map/dot_general | solution.py:67
  32.5 0.1 stack.4
  32.5 9.5 %fusion.6 = f32[112,12,1,896]{3,1,0,2:T(8,128)} fusion(f32[16,112,896]{2,0,1:T(8,128)} %fusion, f32[16,896]{1,0:T(8,128)S(1)} %subtract_divide_fusion, f32[12,16]{1,0:T(8,128)S(1)} %stack.4, f32[16]{0:T(128)S(1)} %get-tuple-element.9), kind=kOutput, calls=%fused_computation.6 | convolution fusion | flops 232816832 | bytes 11297600 | tf_op jit(solution)/shard_map/lg,gakc->alkc/dot_general | solution.py:75
  42.0 0.0 copy-start.2
  42.0 0.0 copy-start.1
  42.0 0.0 reduce-scatter.2.cloned.1.call-update
  42.1 70.5 %reduce-scatter.2.cloned.1.call-done = f32[7,12,1,896]{3,1,0,2:T(8,128)} async-done(((f32[112,12,1,896]{3,1,0,2:T(8,128)}), f32[7,12,1,896]{3,1,0,2:T(8,128)}) %reduce-scatter.2.cloned.1.call-update) | async-done | bytes 301072 | tf_op jit(solution)/shard_map/reduce_scatter | solution.py:74
  112.6 3.7 %stack.5 = f32[8,7,12,1,896]{4,3,2,1,0:T(1,128)} broadcast(f32[7,12,896]{2,1,0:T(8,128)} %bitcast.42), dimensions={1,2,4} | broadcast | bytes 2709504 | tf_op jit(solution)/shard_map/stack | solution.py:8
  116.3 6.5 %all-to-all-start = ((f32[8,7,12,1,896]{4,3,2,1,0:T(1,128)}), f32[8,7,12,1,896]{4,3,2,1,0:T(1,128)S(1)}, u32[]{:S(2)}, u32[]{:S(2)}) async-start(f32[8,7,12,1,896]{4,3,2,1,0:T(1,128)} %stack.5), calls=%async_computation.1 | async-start | bytes 4816896 | tf_op jit(solution)/shard_map/all_to_all | solution.py:7
  122.8 0.0 copy-done.2
  122.8 0.1 dynamic_slice.10
  122.8 0.0 copy-done
  122.8 0.2 fusion.10
  123.0 0.1 copy.18
  123.2 0.0 copy-done.1
  123.2 0.2 fusion.19
  123.4 3.3 %broadcast_in_dim.4 = f32[7,12,112,8]{3,2,0,1:T(8,128)} broadcast(f32[7,12,112]{2,0,1:T(8,128)S(1)} %fusion.19), dimensions={0,1,2} | broadcast | bytes 338688 | tf_op jit(solution)/shard_map/broadcast_in_dim | solution.py:40
  126.7 4.1 %broadcast_in_dim.5 = f32[7,12,896]{2,0,1:T(8,128)S(1)} reshape(f32[7,12,112,8]{3,2,0,1:T(8,128)} %broadcast_in_dim.4) | data formatting | bytes 602112 | tf_op jit(solution)/shard_map/broadcast_in_dim | solution.py:40
  130.8 0.1 copy.29
  130.8 23.8 %all-to-all-done = f32[8,7,12,1,896]{4,3,2,1,0:T(1,128)S(1)} async-done(((f32[8,7,12,1,896]{4,3,2,1,0:T(1,128)}), f32[8,7,12,1,896]{4,3,2,1,0:T(1,128)S(1)}, u32[]{:S(2)}, u32[]{:S(2)}) %all-to-all-start) | async-done | bytes 2408480 | tf_op jit(solution)/shard_map/all_to_all | solution.py:7
  154.6 0.9 fusion.9
  (4 shorter events, 0.1 us)
Async XLA Ops:
  6.5 116.3 %copy-start = (f32[8,12,8,8]{1,3,2,0:T(8,128)S(1)}, f32[8,12,8,8]{1,3,2,0:T(8,128)}, u32[]{:S(2)}) copy-start(f32[8,12,8,8]{1,3,2,0:T(8,128)} %param.11) | copy-start | bytes 73732
  6.5 106.1 %reduce-scatter.2.cloned.1.call-start = ((), (), s32[]{:S(2)}) async-start(), calls=%async_computation.2 | async-start | bytes 6823936 | tf_op jit(solution)/shard_map/reduce_scatter | solution.py:74
  42.0 80.7 %copy-start.2 = (s32[112]{0:T(128)S(1)}, s32[112]{0:T(128)}, u32[]{:S(2)}) copy-start(s32[112]{0:T(128)} %param.9) | copy-start | bytes 1348
  42.0 81.1 %copy-start.1 = (s32[112]{0:T(128)S(1)}, s32[112]{0:T(128)}, u32[]{:S(2)}) copy-start(s32[112]{0:T(128)} %param.10) | copy-start | bytes 1348
  116.3 38.3 %all-to-all-start = ((f32[8,7,12,1,896]{4,3,2,1,0:T(1,128)}), f32[8,7,12,1,896]{4,3,2,1,0:T(1,128)S(1)}, u32[]{:S(2)}, u32[]{:S(2)}) async-start(f32[8,7,12,1,896]{4,3,2,1,0:T(1,128)} %stack.5), calls=%async_computation.1 | async-start | bytes 4816896 | tf_op jit(solution)/shard_map/all_to_all | solution.py:7
Sparse Core Ops, SparseCore 0:
  42.2 70.3 reduce-scatter.1
